TPU v7x, 32 devices: a whole 2x2x4 slice. The times are simulated.
32 devices in a mesh: group: 2 (over x), src: 8 (over z, y), tile: 2 (over core).
Axes of the slice: x: 2, y: 2, z: 4, core: 2. Of those that a mesh axis runs over, the one named last changes fastest.
Arguments:
- near_field: bfloat16 [4, 64, 2, 3, 512], P(('group', 'tile'), 'src'), parts along dimension 0, may hold values from -6 to 6
- x_taps: bfloat16 [8, 2, 8, 65], P('src'), may hold values from -0.5 to 0.5
- y_taps: bfloat16 [8, 2, 8, 65], P('src'), may hold values from -0.1875 to 0.1875
- source_weight: float32 [8], P('src'), may hold values from 0.0125 to 0.125
Outputs:
- intensity: float32 [4, 64, 512], P(('group', 'tile'), 'src'), parts along dimension 0
There are 2 independent parts, one for each index of `group`. A program takes and returns all parts, laid end to end along the dimension named above; an argument that names none is the same for every part. Nothing has to cross between parts.
All inputs are finite; a program needn't handle non-finite values.
Results may differ from a plain program's by a relative error of at most 0.00054.
Values may be sent and summed in bfloat16 or wider, within the bound.
A program may use at most 128 MiB of HBM per device.

v0:
```python
import jax
import jax.numpy as jnp
from jax import lax
from jax.sharding import PartitionSpec as P


def padded_2(cells, sides, width):
    for axis, dim in sides:
        count = lax.axis_size(axis)
        ends = count - 1
        head = lax.slice_in_dim(cells, 0, width, axis=dim)
        tail = lax.slice_in_dim(cells, cells.shape[dim] - width, cells.shape[dim], axis=dim)
        cells = jnp.concatenate(
            [
                lax.ppermute(tail, axis, [(i, (i + 1) % count) for i in range(ends)]),
                cells,
                lax.ppermute(head, axis, [((i + 1) % count, i) for i in range(ends)]),
            ],
            axis=dim,
        )
    return cells


def column_mats(taps):
    tap_count = taps.shape[-1]
    shift = lax.broadcasted_iota(jnp.int32, (tap_count, 256, 128), 0)
    inner = lax.broadcasted_iota(jnp.int32, (tap_count, 256, 128), 1)
    outer = lax.broadcasted_iota(jnp.int32, (tap_count, 256, 128), 2)
    select = (inner - outer == shift).astype(jnp.float32)
    coef = jnp.einsum(
        "xprt,tqj->xpqrj", taps.astype(jnp.float32), select, precision=lax.Precision.HIGHEST
    )
    real_part, imag_part = (coef[:, 0], coef[:, 1])
    full = jnp.stack(
        [jnp.stack([real_part, imag_part], axis=2), jnp.stack([-imag_part, real_part], axis=2)],
        axis=1,
    ).astype(jnp.bfloat16)
    return (full[:, :, :128], full[:, :, 128:])


def column_pass(rows_field, lower_mat, upper_mat, rim_width):
    count_rows, _, comps, width = rows_field.shape
    padded = jnp.pad(rows_field, ((0, 0), (0, 0), (0, 0), (rim_width, 128 - rim_width)))
    pieces = padded.reshape(count_rows, 2, comps, width // 128 + 1, 128)
    result = jnp.einsum(
        "ipcbq,xpqsrj->ixsrcbj", pieces[:, :, :, :-1], lower_mat, preferred_element_type=jnp.float32
    )
    result = result + jnp.einsum(
        "ipcbq,xpqsrj->ixsrcbj", pieces[:, :, :, 1:], upper_mat, preferred_element_type=jnp.float32
    )
    sources, ranks = (lower_mat.shape[0], lower_mat.shape[4])
    return result.reshape(count_rows, sources, 2, ranks, comps, width).astype(jnp.bfloat16)


def row_matrices(taps, block_rows, rim_width):
    tap_count = taps.shape[-1]
    span = block_rows + 2 * rim_width
    shift = lax.broadcasted_iota(jnp.int32, (tap_count, block_rows, span), 0)
    out_row = lax.broadcasted_iota(jnp.int32, (tap_count, block_rows, span), 1)
    in_row = lax.broadcasted_iota(jnp.int32, (tap_count, block_rows, span), 2)
    select = (in_row - out_row == shift).astype(jnp.float32)
    coef = jnp.einsum(
        "xprt,tik->xpirk", taps.astype(jnp.float32), select, precision=lax.Precision.HIGHEST
    )
    real_part, imag_part = (coef[:, 0], coef[:, 1])
    full = jnp.stack(
        [jnp.stack([real_part, -imag_part], axis=2), jnp.stack([imag_part, real_part], axis=2)],
        axis=1,
    )
    return full.astype(jnp.bfloat16)


def per_device(near_field, x_taps, y_taps, source_weight):
    rim_width = (x_taps.shape[-1] - 1) // 2
    width = near_field.shape[-1]
    local_rows = near_field.shape[1]
    whole_tile = lax.all_gather(near_field, "src", axis=1, tiled=True)
    padded_field = padded_2(whole_tile, (("tile", 1),), rim_width)
    lower_mat, upper_mat = column_mats(x_taps)
    padded_pass = column_pass(padded_field[0], lower_mat, upper_mat, rim_width)
    tile_rows = padded_pass.shape[0] - 2 * rim_width
    block_rows = 64
    row_mats = row_matrices(y_taps, block_rows, rim_width)

    def one_block(index):
        first_row = index * block_rows
        window = lax.dynamic_slice_in_dim(padded_pass, first_row, block_rows + 2 * rim_width, 0)
        image = jnp.einsum(
            "xoiprk,kxprcw->xoicw", row_mats, window, preferred_element_type=jnp.float32
        )
        power = jnp.sum(image * image, axis=(1, 3))
        return jnp.sum(source_weight[:, None, None] * power, axis=0)

    blocks = lax.map(one_block, jnp.arange(tile_rows // block_rows, dtype=jnp.int32))
    own_image = blocks.reshape(tile_rows, width)
    summed = lax.psum_scatter(own_image, "src", scatter_dimension=0, tiled=True)
    return summed.reshape(1, local_rows, width)


def solution(mesh):
    placed = (
        P(("group", "tile"), "src", None, None, None),
        P("src", None, None, None),
        P("src", None, None, None),
        P("src"),
    )
    return jax.shard_map(
        per_device,
        mesh=mesh,
        in_specs=placed,
        out_specs=P(("group", "tile"), "src", None),
        check_vma=False,
    )
```

profile of v0, /device:TPU:0, one launch (start us, length us, event | category | flops | bytes accessed | tf_op | source)
XLA Modules:
  0.0 142.8 jit_solution(395169081686979123)
XLA Ops:
  6.5 0.0 copy-start
  6.5 33.1 %all_gather.3 = bf16[1,64,2,3,512]{4,2,3,0,1:T(2,128)(2,1)S(1)} all-gather(bf16[1,8,2,3,512]{4,2,3,0,1:T(2,128)(2,1)} %bitcast.120), channel_id=1, replica_groups=mesh['group'=2,'src'=8,'tile'=2] {'src'}, dimensions={1}, use_global_device_ids=true | all-gather | bytes 442368 | tf_op jit(solution)/shard_map/all_gather | solution.py:77
  39.6 0.3 fusion.45
  39.9 0.7 copy.29
  40.6 2.0 %collective-permute-start = (bf16[1,32,2,3,512]{4,1,3,2,0:T(8,128)(2,1)}, bf16[1,32,2,3,512]{4,1,3,2,0:T(8,128)(2,1)}, u32[]{:S(2)}, u32[]{:S(2)}) collective-permute-start(bf16[1,32,2,3,512]{4,1,3,2,0:T(8,128)(2,1)} %copy.29), channel_id=1, source_target_pairs={{0,1},{2,3},{4,5},{6,7},{8,9},{10,11},{12,13},{14,15},{16,17},{18,... | collective-permute-start | bytes 589832 | tf_op jit(solution)/shard_map/ppermute | solution.py:15
  42.6 0.7 copy.30
  43.3 1.3 collective-permute-start.1
  44.6 0.0 copy-done
  44.6 1.1 fusion.9
  45.7 0.1 fusion.36
  45.9 0.1 fusion.35
  45.9 0.5 copy-done.2
  46.4 0.5 fusion.18
  47.0 1.1 maximum_bitcast_fusion.1
  48.1 0.8 maximum_bitcast_fusion.3
  49.0 1.3 copy.32
  50.9 1.4 fusion.26
  52.3 0.0 collective-permute-done
  52.3 2.2 %copy.31 = bf16[1,32,2,3,512]{1,4,3,2,0:T(8,128)(2,1)} copy(bf16[1,32,2,3,512]{4,1,3,2,0:T(8,128)(2,1)} %collective-permute-done) | data formatting | bytes 393216 | tf_op jit(solution)/shard_map/ppermute | solution.py:15
  54.5 0.0 collective-permute-done.1
  54.5 2.1 %copy.33 = bf16[1,32,2,3,512]{1,4,3,2,0:T(8,128)(2,1)} copy(bf16[1,32,2,3,512]{4,1,3,2,0:T(8,128)(2,1)} %collective-permute-done.1) | data formatting | bytes 393216 | tf_op jit(solution)/shard_map/ppermute | solution.py:17
  56.6 2.1 %maximum_bitcast_fusion.2 = bf16[128,2,3,512]{0,3,2,1:T(8,128)(2,1)S(1)} fusion(bf16[1,32,2,3,512]{1,4,3,2,0:T(8,128)(2,1)} %copy.33, bf16[1,64,2,3,512]{1,4,3,2,0:T(8,128)(2,1)S(1)} %copy-done.1, bf16[1,32,2,3,512]{1,4,3,2,0:T(8,128)(2,1)} %copy.31), kind=kLoop, calls=%fused_computation.31 | loop fusion | flops 2359296 | bytes 1572864 | tf_op jit(solution)/shard_map/squeeze | solution.py:80
  58.7 0.1 pad.4
  58.8 1.1 fusion.44
  59.9 1.2 copy.61
  61.1 1.5 %copy.62 = bf16[128,2,3,4,128]{4,0,1,3,2:T(8,128)(2,1)S(1)} copy(bf16[128,2,3,4,128]{0,4,3,2,1:T(8,128)(2,1)} %get-tuple-element.24) | data formatting | bytes 1572864
  62.6 3.0 %fusion.29 = f32[2,8,128,128,3,4,1]{3,2,6,5,4,1,0:T(8,128)S(1)} fusion(bf16[2,128,2,8,128,1,1]{4,3,1,2,0,6,5:T(8,128)(2,1)S(1)} %get-tuple-element.14, bf16[128,2,3,4,128]{4,0,1,3,2:T(8,128)(2,1)} %copy.61), kind=kOutput, calls=%fused_computation.26 | convolution fusion | flops 1610612736 | bytes 14417920 | tf_op jit(solution)/shard_map/ipcbq,xpqsrj->ixsrcbj/dot_general | solution.py:45
  65.6 2.3 %fusion = bf16[2,8,128,128,3,4]{3,2,5,4,1,0:T(8,128)(2,1)S(1)} fusion(f32[2,8,128,128,3,4,1]{3,2,6,5,4,1,0:T(8,128)S(1)} %fusion.29, bf16[2,128,2,8,128,1,1]{4,3,1,2,0,6,5:T(8,128)(2,1)S(1)} %get-tuple-element.13, bf16[128,2,3,4,128]{4,0,1,3,2:T(8,128)(2,1)S(1)} %copy.62), kind=kOutput, calls=%fused_computation.1 | convolution fusion | flops 1616904192 | bytes 20709376 | tf_op jit(solution)/shard_map/ipcbq,xpqsrj->ixsrcbj/dot_general | solution.py:48
  67.9 3.2 %fusion.21 = f32[64,512]{1,0:T(8,128)S(1)} fusion(bf16[128,2,8,3,512,1]{0,4,3,2,1,5:T(8,128)(2,1)S(1)} %bitcast.119, bf16[2,64,2,8,128,1]{4,3,1,2,0,5:T(8,128)(2,1)} %maximum_bitcast_fusion.3), kind=kOutput, calls=%fused_computation.16 | convolution fusion | flops 805666816 | bytes 6946816 | tf_op jit(solution)/shard_map/while/body/eval_jaxpr/xoiprk,kxprcw->xoicw/dot_general | solution.py:88
  71.1 0.7 broadcast_multiply_fusion
  71.8 0.0 reduce-scatter.2.cloned.1.call-update
  71.8 64.1 %reduce-scatter.2.cloned.1.call-done = f32[8,512]{1,0:T(8,128)} async-done(((f32[64,512]{1,0:T(8,128)}), f32[8,512]{1,0:T(8,128)}) %reduce-scatter.2.cloned.1.call-update) | async-done | bytes 16400 | tf_op jit(solution)/shard_map/reduce_scatter | solution.py:96
  (6 shorter events, 0.1 us)
Async XLA Ops:
  6.5 38.0 %copy-start = (bf16[1,2,8,65]{3,2,1,0:T(8,128)(2,1)S(1)}, bf16[1,2,8,65]{3,2,1,0:T(8,128)(2,1)}, u32[]{:S(2)}) copy-start(bf16[1,2,8,65]{3,2,1,0:T(8,128)(2,1)} %param.5) | copy-start | bytes 6244
  6.5 129.4 %reduce-scatter.2.cloned.1.call-start = ((), (), s32[]{:S(2)}) async-start(), calls=%async_computation.1 | async-start | bytes 147456 | tf_op jit(solution)/shard_map/reduce_scatter | solution.py:96
  40.6 11.8 %collective-permute-start = (bf16[1,32,2,3,512]{4,1,3,2,0:T(8,128)(2,1)}, bf16[1,32,2,3,512]{4,1,3,2,0:T(8,128)(2,1)}, u32[]{:S(2)}, u32[]{:S(2)}) collective-permute-start(bf16[1,32,2,3,512]{4,1,3,2,0:T(8,128)(2,1)} %copy.29), channel_id=1, source_target_pairs={{0,1},{2,3},{4,5},{6,7},{8,9},{10,11},{12,13},{14,15},{16,17},{18,... | collective-permute-start | bytes 589832 | tf_op jit(solution)/shard_map/ppermute | solution.py:15
  43.3 11.2 %collective-permute-start.1 = (bf16[1,32,2,3,512]{4,1,3,2,0:T(8,128)(2,1)}, bf16[1,32,2,3,512]{4,1,3,2,0:T(8,128)(2,1)}, u32[]{:S(2)}, u32[]{:S(2)}) collective-permute-start(bf16[1,32,2,3,512]{4,1,3,2,0:T(8,128)(2,1)} %copy.30), channel_id=1, source_target_pairs={{1,0},{3,2},{5,4},{7,6},{9,8},{11,10},{13,12},{15,14},{17,16},{19,... | collective-permute-start | bytes 589832 | tf_op jit(solution)/shard_map/ppermute | solution.py:17
  45.7 0.7 copy-start.2
  52.3 4.3 %copy-start.1 = (bf16[1,64,2,3,512]{1,4,3,2,0:T(8,128)(2,1)S(1)}, bf16[1,64,2,3,512]{1,4,3,2,0:T(8,128)(2,1)}, u32[]{:S(2)}) copy-start(bf16[1,64,2,3,512]{1,4,3,2,0:T(8,128)(2,1)} %copy.32) | copy-start | bytes 1179652
Sparse Core Ops, SparseCore 0:
  71.9 63.9 reduce-scatter.1
where the time goes:
time: 143 us
  waiting for transfers between devices  64.1 us (45%)
  blocking collectives  33.1 us (23%)
  between operations  14.2 us (10%)
  local copies, waits for them, and re-layouts  11.8 us (8%)
  matrix products  10.1 us (7%)
  other arithmetic  6.23 us (4%)
  starting transfers between devices  3.26 us (2%)
    reduce_scatter x1, waiting for transfers between devices, per_device(): summed = lax.psum_scatter(own_image, 'src', scatter_dimension=0, tiled=True)  64.1 us
    all_gather x1, blocking collectives, per_device(): whole_tile = lax.all_gather(near_field, 'src', axis=1, tiled=True)  33.1 us
    dot_general x1, matrix products, one_block(): jnp.einsum('xoiprk,kxprcw->xoicw', row_mats, window, preferred_element_ty...  3.22 us
    unnamed x8, local copies, waits for them, and re-layouts  3.17 us
    dot_general x1, matrix products, column_pass(): jnp.einsum('ipcbq,xpqsrj->ixsrcbj', pieces[:, :, :, :-1], lower_mat, pref...  2.99 us
  transfers between devices with their start and end apart: 3, of which 1 were waited for; matrix products, arithmetic and copies ran while one was open for 7% of the time, Pallas kernels for 0%

commit v1 on v0

--- a/solution.py
+++ b/solution.py
@@ -74,7 +74,25 @@
     rim_width = (x_taps.shape[-1] - 1) // 2
     width = near_field.shape[-1]
     local_rows = near_field.shape[1]
-    whole_tile = lax.all_gather(near_field, "src", axis=1, tiled=True)
+    size, here, span_2 = (lax.axis_size("src"), lax.axis_index("src"), near_field.shape[1])
+    right = [(i_2, (i_2 + 1) % size) for i_2 in range(size)]
+    left = [(i_2, (i_2 - 1) % size) for i_2 in range(size)]
+    whole_tile = jnp.zeros(
+        (*near_field.shape[:1], size * span_2, *near_field.shape[1 + 1 :]), near_field.dtype
+    )
+    whole_tile = lax.dynamic_update_slice_in_dim(whole_tile, near_field, here * span_2, axis=1)
+    from_left = from_right = near_field
+    half = size // 2
+    for step in range(1, half + 1):
+        from_left = lax.ppermute(from_left, "src", right)
+        whole_tile = lax.dynamic_update_slice_in_dim(
+            whole_tile, from_left, (here - step) % size * span_2, axis=1
+        )
+        if step < size - half:
+            from_right = lax.ppermute(from_right, "src", left)
+            whole_tile = lax.dynamic_update_slice_in_dim(
+                whole_tile, from_right, (here + step) % size * span_2, axis=1
+            )
     padded_field = padded_2(whole_tile, (("tile", 1),), rim_width)
     lower_mat, upper_mat = column_mats(x_taps)
     padded_pass = column_pass(padded_field[0], lower_mat, upper_mat, rim_width)

time: 143 us -> 172 us (1.20)
  local copies, waits for them, and re-layouts: 11.8 us -> 54 us
  blocking collectives: 33.1 us -> 0 us
  starting transfers between devices: 3.26 us -> 19.3 us
  waiting for transfers between devices: 64.1 us -> 67.5 us
    dynamic_update_slice x0 -> x8, local copies, waits for them, and re-layouts: none -> 37.7 us  [the longest x4 20.1 us: per_device(): lax.dynamic_update_slice_in_dim(whole_tile, from_left, (here - step) % si...]
    all_gather x1 -> x0, blocking collectives: 33.1 us -> none  [per_device(): whole_tile = lax.all_gather(near_field, 'src', axis=1, tiled=True)]
    ppermute x0 -> x7, starting transfers between devices: none -> 15.9 us  [the longest x3 12.8 us: per_device(): from_right = lax.ppermute(from_right, 'src', left)]
    ppermute x0 -> x7, waiting for transfers between devices: none -> 3.06 us  [the longest x4 2.66 us: per_device(): from_left = lax.ppermute(from_left, 'src', right)]
    ppermute x0 -> x7, local copies, waits for them, and re-layouts: none -> 2.59 us  [the longest x4 1.48 us: per_device(): from_left = lax.ppermute(from_left, 'src', right)]
    unnamed x8 -> x12, local copies, waits for them, and re-layouts: 3.17 us -> 5.52 us
  transfers between devices with their start and end apart: 3 -> 10, of which waited for: 1 -> 4; matrix products, arithmetic and copies ran while one was open for 7% -> 26% of each run, Pallas kernels for 0% -> 0%
where the time goes in v1:
time: 172 us
  waiting for transfers between devices  67.5 us (39%)
  local copies, waits for them, and re-layouts  54 us (31%)
  starting transfers between devices  19.3 us (11%)
  between operations  14.4 us (8%)
  matrix products  9 us (5%)
  other arithmetic  7.28 us (4%)
    reduce_scatter x1, waiting for transfers between devices, per_device(): summed = lax.psum_scatter(own_image, 'src', scatter_dimension=0, tiled=True)  64.4 us
    dynamic_update_slice x4, local copies, waits for them, and re-layouts, per_device(): lax.dynamic_update_slice_in_dim(whole_tile, from_left, (here - step) % si...  20.1 us
    dynamic_update_slice x3, local copies, waits for them, and re-layouts, per_device(): lax.dynamic_update_slice_in_dim(whole_tile, from_right, (here + step) % s...  15.1 us
    ppermute x3, starting transfers between devices, per_device(): from_right = lax.ppermute(from_right, 'src', left)  12.8 us
    unnamed x12, local copies, waits for them, and re-layouts  5.52 us
  transfers between devices with their start and end apart: 10, of which 4 were waited for; matrix products, arithmetic and copies ran while one was open for 26% of the time, Pallas kernels for 0%

profile of v1, /device:TPU:0, one launch (start us, length us, event | category | flops | bytes accessed | tf_op | source)
XLA Modules:
  0.0 171.5 jit_solution(4542771930146322577)
XLA Ops:
  7.4 3.0 %collective-permute-start = (bf16[1,8,2,3,512]{4,1,3,2,0:T(8,128)(2,1)S(1)}, bf16[1,8,2,3,512]{4,1,3,2,0:T(8,128)(2,1)S(1)}, u32[]{:S(2)}, u32[]{:S(2)}) collective-permute-start(bf16[1,8,2,3,512]{4,1,3,2,0:T(8,128)(2,1)S(1)} %copy.31), channel_id=1, source_target_pairs={{0,2},{2,4},{4,6},{6,8},{8,10},{10,12},{12,14},{14,0},{1,3},{3,5},... | collective-permute-start | bytes 147464 | tf_op jit(solution)/shard_map/ppermute | solution.py:87
  10.3 3.1 %collective-permute-start.1 = (bf16[1,8,2,3,512]{4,1,3,2,0:T(8,128)(2,1)S(1)}, bf16[1,8,2,3,512]{4,1,3,2,0:T(8,128)(2,1)S(1)}, u32[]{:S(2)}, u32[]{:S(2)}) collective-permute-start(bf16[1,8,2,3,512]{4,1,3,2,0:T(8,128)(2,1)S(1)} %copy.31), channel_id=1, source_target_pairs={{0,14},{2,0},{4,2},{6,4},{8,6},{10,8},{12,10},{14,12},{1,15},{3,1}... | collective-permute-start | bytes 147464 | tf_op jit(solution)/shard_map/ppermute | solution.py:92
  13.4 1.1 fusion.9
  16.6 4.7 %collective-permute-start.3 = (bf16[1,8,2,3,512]{4,1,3,2,0:T(8,128)(2,1)S(1)}, bf16[1,8,2,3,512]{4,1,3,2,0:T(8,128)(2,1)S(1)}, u32[]{:S(2)}, u32[]{:S(2)}) collective-permute-start(bf16[1,8,2,3,512]{4,1,3,2,0:T(8,128)(2,1)S(1)} %collective-permute-done.1), channel_id=1, source_target_pairs={{0,14},{2,0},{4,2},{6,4},{8,6},{10,8},{12,10},{14,12},{1,15},{3,1}... | collective-permute-start | bytes 147464 | tf_op jit(solution)/shard_map/ppermute | solution.py:92
  21.3 1.3 collective-permute-done.2
  23.0 5.0 %collective-permute-start.5 = (bf16[1,8,2,3,512]{4,1,3,2,0:T(8,128)(2,1)S(1)}, bf16[1,8,2,3,512]{4,1,3,2,0:T(8,128)(2,1)S(1)}, u32[]{:S(2)}, u32[]{:S(2)}) collective-permute-start(bf16[1,8,2,3,512]{4,1,3,2,0:T(8,128)(2,1)S(1)} %collective-permute-done.3), channel_id=1, source_target_pairs={{0,14},{2,0},{4,2},{6,4},{8,6},{10,8},{12,10},{14,12},{1,15},{3,1}... | collective-permute-start | bytes 147464 | tf_op jit(solution)/shard_map/ppermute | solution.py:92
  28.1 1.3 collective-permute-done.4
  29.4 1.2 maximum_bitcast_fusion.1
  31.2 2.5 %dynamic_update_slice.27 = bf16[1,64,2,3,512]{1,4,3,2,0:T(8,128)(2,1)S(1)} dynamic-update-slice(bf16[1,64,2,3,512]{1,4,3,2,0:T(8,128)(2,1)S(1)} %broadcast_in_dim.9, bf16[1,8,2,3,512]{1,4,3,2,0:T(8,128)(2,1)S(1)} %copy.30, s32[]{:T(128)} %constant.67.clone.1, s32[]{:T(128)S(6)} %select_n.57, s32[]{:T(128)} %constant.67.clone.1, s32[]{:T(128)} %constant.67.clone.1, s32[]{:T(128)} %constant.67.clone.1) | dynamic-update-slice | bytes 98308 | tf_op jit(solution)/shard_map/dynamic_update_slice | solution.py:83
  34.1 5.0 %dynamic_update_slice.28 = bf16[1,64,2,3,512]{1,4,3,2,0:T(8,128)(2,1)S(1)} dynamic-update-slice(bf16[1,64,2,3,512]{1,4,3,2,0:T(8,128)(2,1)S(1)} %dynamic_update_slice.27, bf16[1,8,2,3,512]{1,4,3,2,0:T(8,128)(2,1)S(1)} %copy.32, s32[]{:T(128)} %constant.67.clone.1, s32[]{:T(128)S(6)} %select_n.59, s32[]{:T(128)} %constant.67.clone.1, s32[]{:T(128)} %constant.67.clone.1, s32[]{:T(128)} %constant.67.clone.1) | dynamic-update-slice | bytes 98308 | tf_op jit(solution)/shard_map/dynamic_update_slice | solution.py:88
  39.5 5.0 %dynamic_update_slice.29 = bf16[1,64,2,3,512]{1,4,3,2,0:T(8,128)(2,1)S(1)} dynamic-update-slice(bf16[1,64,2,3,512]{1,4,3,2,0:T(8,128)(2,1)S(1)} %dynamic_update_slice.28, bf16[1,8,2,3,512]{1,4,3,2,0:T(8,128)(2,1)S(1)} %copy.34, s32[]{:T(128)} %constant.67.clone.1, s32[]{:T(128)S(6)} %select_n.61, s32[]{:T(128)} %constant.67.clone.1, s32[]{:T(128)} %constant.67.clone.1, s32[]{:T(128)} %constant.67.clone.1) | dynamic-update-slice | bytes 98308 | tf_op jit(solution)/shard_map/dynamic_update_slice | solution.py:93
  44.9 5.0 %dynamic_update_slice.30 = bf16[1,64,2,3,512]{1,4,3,2,0:T(8,128)(2,1)S(1)} dynamic-update-slice(bf16[1,64,2,3,512]{1,4,3,2,0:T(8,128)(2,1)S(1)} %dynamic_update_slice.29, bf16[1,8,2,3,512]{1,4,3,2,0:T(8,128)(2,1)S(1)} %copy.35, s32[]{:T(128)} %constant.67.clone.1, s32[]{:T(128)S(6)} %select_n.63, s32[]{:T(128)} %constant.67.clone.1, s32[]{:T(128)} %constant.67.clone.1, s32[]{:T(128)} %constant.67.clone.1) | dynamic-update-slice | bytes 98308 | tf_op jit(solution)/shard_map/dynamic_update_slice | solution.py:88
  50.3 5.0 %dynamic_update_slice.31 = bf16[1,64,2,3,512]{1,4,3,2,0:T(8,128)(2,1)S(1)} dynamic-update-slice(bf16[1,64,2,3,512]{1,4,3,2,0:T(8,128)(2,1)S(1)} %dynamic_update_slice.30, bf16[1,8,2,3,512]{1,4,3,2,0:T(8,128)(2,1)S(1)} %copy.36, s32[]{:T(128)} %constant.67.clone.1, s32[]{:T(128)S(6)} %select_n.65, s32[]{:T(128)} %constant.67.clone.1, s32[]{:T(128)} %constant.67.clone.1, s32[]{:T(128)} %constant.67.clone.1) | dynamic-update-slice | bytes 98308 | tf_op jit(solution)/shard_map/dynamic_update_slice | solution.py:93
  55.8 5.0 %dynamic_update_slice.32 = bf16[1,64,2,3,512]{1,4,3,2,0:T(8,128)(2,1)S(1)} dynamic-update-slice(bf16[1,64,2,3,512]{1,4,3,2,0:T(8,128)(2,1)S(1)} %dynamic_update_slice.31, bf16[1,8,2,3,512]{1,4,3,2,0:T(8,128)(2,1)S(1)} %copy.37, s32[]{:T(128)} %constant.67.clone.1, s32[]{:T(128)S(6)} %select_n.67, s32[]{:T(128)} %constant.67.clone.1, s32[]{:T(128)} %constant.67.clone.1, s32[]{:T(128)} %constant.67.clone.1) | dynamic-update-slice | bytes 98308 | tf_op jit(solution)/shard_map/dynamic_update_slice | solution.py:88
  61.2 5.0 %dynamic_update_slice.33 = bf16[1,64,2,3,512]{1,4,3,2,0:T(8,128)(2,1)S(1)} dynamic-update-slice(bf16[1,64,2,3,512]{1,4,3,2,0:T(8,128)(2,1)S(1)} %dynamic_update_slice.32, bf16[1,8,2,3,512]{1,4,3,2,0:T(8,128)(2,1)S(1)} %copy.38, s32[]{:T(128)} %constant.67.clone.1, s32[]{:T(128)S(6)} %select_n.69, s32[]{:T(128)} %constant.67.clone.1, s32[]{:T(128)} %constant.67.clone.1, s32[]{:T(128)} %constant.67.clone.1) | dynamic-update-slice | bytes 98308 | tf_op jit(solution)/shard_map/dynamic_update_slice | solution.py:93
  66.6 5.0 %dynamic_update_slice.34 = bf16[1,64,2,3,512]{1,4,3,2,0:T(8,128)(2,1)S(1)} dynamic-update-slice(bf16[1,64,2,3,512]{1,4,3,2,0:T(8,128)(2,1)S(1)} %dynamic_update_slice.33, bf16[1,8,2,3,512]{1,4,3,2,0:T(8,128)(2,1)S(1)} %copy.39, s32[]{:T(128)} %constant.67.clone.1, s32[]{:T(128)S(6)} %select_n.71, s32[]{:T(128)} %constant.67.clone.1, s32[]{:T(128)} %constant.67.clone.1, s32[]{:T(128)} %constant.67.clone.1) | dynamic-update-slice | bytes 98308 | tf_op jit(solution)/shard_map/dynamic_update_slice | solution.py:88
  71.9 0.9 copy.40
  72.9 2.0 %collective-permute-start.7 = (bf16[1,32,2,3,512]{4,1,3,2,0:T(8,128)(2,1)}, bf16[1,32,2,3,512]{4,1,3,2,0:T(8,128)(2,1)}, u32[]{:S(2)}, u32[]{:S(2)}) collective-permute-start(bf16[1,32,2,3,512]{4,1,3,2,0:T(8,128)(2,1)} %copy.40), channel_id=1, source_target_pairs={{0,1},{2,3},{4,5},{6,7},{8,9},{10,11},{12,13},{14,15},{16,17},{18,... | collective-permute-start | bytes 589832 | tf_op jit(solution)/shard_map/ppermute | solution.py:15
  74.9 0.9 copy.41
  75.8 1.5 collective-permute-start.8
  77.3 1.1 maximum_bitcast_fusion.3
  79.0 2.4 %fusion.26 = (bf16[2,128,2,8,128,1,1]{4,3,1,2,0,6,5:T(8,128)(2,1)}, bf16[2,128,2,8,128,1,1]{4,3,1,2,0,6,5:T(8,128)(2,1)S(1)}) fusion(bf16[1,1,256,2,8,128]{5,4,2,3,1,0:T(8,128)(2,1)S(1)} %get-tuple-element.30, bf16[1,1,256,2,8,128]{5,4,2,3,1,0:T(8,128)(2,1)} %get-tuple-element.31), kind=kLoop, calls=%fused_computation.20 | loop fusion | flops 1048576 | bytes 4194304 | tf_op jit(solution)/shard_map/reshape.11
  81.4 1.3 copy.42
  82.7 2.1 %copy.43 = bf16[1,32,2,3,512]{1,4,3,2,0:T(8,128)(2,1)} copy(bf16[1,32,2,3,512]{4,1,3,2,0:T(8,128)(2,1)} %collective-permute-done.8) | data formatting | bytes 393216 | tf_op jit(solution)/shard_map/ppermute | solution.py:17
  84.8 1.9 %maximum_bitcast_fusion.2 = bf16[128,2,3,512]{0,3,2,1:T(8,128)(2,1)S(1)} fusion(bf16[1,32,2,3,512]{1,4,3,2,0:T(8,128)(2,1)} %copy.43, bf16[1,64,2,3,512]{1,4,3,2,0:T(8,128)(2,1)S(1)} %dynamic_update_slice.34, bf16[1,32,2,3,512]{1,4,3,2,0:T(8,128)(2,1)S(1)} %copy.42), kind=kLoop, calls=%fused_computation.31 | loop fusion | flops 2359296 | bytes 1572864 | tf_op jit(solution)/shard_map/squeeze | solution.py:98
  86.8 1.5 fusion.44
  88.4 1.5 copy.71
  89.9 2.3 %copy.72 = bf16[128,2,3,4,128]{4,0,1,3,2:T(8,128)(2,1)} copy(bf16[128,2,3,4,128]{0,4,3,2,1:T(8,128)(2,1)} %get-tuple-element.24) | data formatting | bytes 1572864
  92.2 1.9 %fusion.29 = f32[2,8,128,128,3,4,1]{3,2,6,5,4,1,0:T(8,128)S(1)} fusion(bf16[2,128,2,8,128,1,1]{4,3,1,2,0,6,5:T(8,128)(2,1)S(1)} %get-tuple-element.14, bf16[128,2,3,4,128]{4,0,1,3,2:T(8,128)(2,1)S(1)} %copy.71), kind=kOutput, calls=%fused_computation.26 | convolution fusion | flops 1610612736 | bytes 14417920 | tf_op jit(solution)/shard_map/ipcbq,xpqsrj->ixsrcbj/dot_general | solution.py:45
  94.1 3.3 %fusion = bf16[2,8,128,128,3,4]{3,2,5,4,1,0:T(8,128)(2,1)S(1)} fusion(f32[2,8,128,128,3,4,1]{3,2,6,5,4,1,0:T(8,128)S(1)} %fusion.29, bf16[2,128,2,8,128,1,1]{4,3,1,2,0,6,5:T(8,128)(2,1)S(1)} %copy-done.1, bf16[128,2,3,4,128]{4,0,1,3,2:T(8,128)(2,1)} %copy.72), kind=kOutput, calls=%fused_computation.1 | convolution fusion | flops 1616904192 | bytes 20709376 | tf_op jit(solution)/shard_map/ipcbq,xpqsrj->ixsrcbj/dot_general | solution.py:48
  97.4 2.2 %fusion.21 = f32[64,512]{1,0:T(8,128)S(1)} fusion(bf16[128,2,8,3,512,1]{0,4,3,2,1,5:T(8,128)(2,1)S(1)} %bitcast.118, bf16[2,64,2,8,128,1]{4,3,1,2,0,5:T(8,128)(2,1)S(1)} %maximum_bitcast_fusion.3), kind=kOutput, calls=%fused_computation.16 | convolution fusion | flops 805666816 | bytes 6946816 | tf_op jit(solution)/shard_map/while/body/eval_jaxpr/xoiprk,kxprcw->xoicw/dot_general | solution.py:106
  100.3 64.4 %reduce-scatter.2.cloned.1.call-done = f32[8,512]{1,0:T(8,128)} async-done(((f32[64,512]{1,0:T(8,128)}), f32[8,512]{1,0:T(8,128)}) %reduce-scatter.2.cloned.1.call-update) | async-done | bytes 16400 | tf_op jit(solution)/shard_map/reduce_scatter | solution.py:114
  (38 shorter events, 7.4 us)
Async XLA Ops:
  6.5 6.9 %copy-start = (bf16[1,2,8,65]{3,2,1,0:T(8,128)(2,1)S(1)}, bf16[1,2,8,65]{3,2,1,0:T(8,128)(2,1)}, u32[]{:S(2)}) copy-start(bf16[1,2,8,65]{3,2,1,0:T(8,128)(2,1)} %param.5) | copy-start | bytes 6244
  6.5 158.2 %reduce-scatter.2.cloned.1.call-start = ((), (), s32[]{:S(2)}) async-start(), calls=%async_computation.1 | async-start | bytes 147456 | tf_op jit(solution)/shard_map/reduce_scatter | solution.py:114
  7.4 8.4 %collective-permute-start = (bf16[1,8,2,3,512]{4,1,3,2,0:T(8,128)(2,1)S(1)}, bf16[1,8,2,3,512]{4,1,3,2,0:T(8,128)(2,1)S(1)}, u32[]{:S(2)}, u32[]{:S(2)}) collective-permute-start(bf16[1,8,2,3,512]{4,1,3,2,0:T(8,128)(2,1)S(1)} %copy.31), channel_id=1, source_target_pairs={{0,2},{2,4},{4,6},{6,8},{8,10},{10,12},{12,14},{14,0},{1,3},{3,5},... | collective-permute-start | bytes 147464 | tf_op jit(solution)/shard_map/ppermute | solution.py:87
  10.3 6.2 %collective-permute-start.1 = (bf16[1,8,2,3,512]{4,1,3,2,0:T(8,128)(2,1)S(1)}, bf16[1,8,2,3,512]{4,1,3,2,0:T(8,128)(2,1)S(1)}, u32[]{:S(2)}, u32[]{:S(2)}) collective-permute-start(bf16[1,8,2,3,512]{4,1,3,2,0:T(8,128)(2,1)S(1)} %copy.31), channel_id=1, source_target_pairs={{0,14},{2,0},{4,2},{6,4},{8,6},{10,8},{12,10},{14,12},{1,15},{3,1}... | collective-permute-start | bytes 147464 | tf_op jit(solution)/shard_map/ppermute | solution.py:92
  14.6 0.7 copy-start.3
  15.8 14.8 %copy-start.2 = (bf16[1,8,2,3,512]{4,2,3,1,0:T(2,128)(2,1)S(1)}, bf16[1,8,2,3,512]{4,2,3,1,0:T(2,128)(2,1)}, u32[]{:S(2)}) copy-start(bf16[1,8,2,3,512]{4,2,3,1,0:T(2,128)(2,1)} %param.4) | copy-start | bytes 147460
  15.8 6.8 %collective-permute-start.2 = (bf16[1,8,2,3,512]{4,1,3,2,0:T(8,128)(2,1)S(1)}, bf16[1,8,2,3,512]{4,1,3,2,0:T(8,128)(2,1)S(1)}, u32[]{:S(2)}, u32[]{:S(2)}) collective-permute-start(bf16[1,8,2,3,512]{4,1,3,2,0:T(8,128)(2,1)S(1)} %collective-permute-done), channel_id=1, source_target_pairs={{0,2},{2,4},{4,6},{6,8},{8,10},{10,12},{12,14},{14,0},{1,3},{3,5},... | collective-permute-start | bytes 147464 | tf_op jit(solution)/shard_map/ppermute | solution.py:87
  16.6 6.5 %collective-permute-start.3 = (bf16[1,8,2,3,512]{4,1,3,2,0:T(8,128)(2,1)S(1)}, bf16[1,8,2,3,512]{4,1,3,2,0:T(8,128)(2,1)S(1)}, u32[]{:S(2)}, u32[]{:S(2)}) collective-permute-start(bf16[1,8,2,3,512]{4,1,3,2,0:T(8,128)(2,1)S(1)} %collective-permute-done.1), channel_id=1, source_target_pairs={{0,14},{2,0},{4,2},{6,4},{8,6},{10,8},{12,10},{14,12},{1,15},{3,1}... | collective-permute-start | bytes 147464 | tf_op jit(solution)/shard_map/ppermute | solution.py:92
  22.6 6.8 %collective-permute-start.4 = (bf16[1,8,2,3,512]{4,1,3,2,0:T(8,128)(2,1)S(1)}, bf16[1,8,2,3,512]{4,1,3,2,0:T(8,128)(2,1)S(1)}, u32[]{:S(2)}, u32[]{:S(2)}) collective-permute-start(bf16[1,8,2,3,512]{4,1,3,2,0:T(8,128)(2,1)S(1)} %collective-permute-done.2), channel_id=1, source_target_pairs={{0,2},{2,4},{4,6},{6,8},{8,10},{10,12},{12,14},{14,0},{1,3},{3,5},... | collective-permute-start | bytes 147464 | tf_op jit(solution)/shard_map/ppermute | solution.py:87
  23.0 37.8 %collective-permute-start.5 = (bf16[1,8,2,3,512]{4,1,3,2,0:T(8,128)(2,1)S(1)}, bf16[1,8,2,3,512]{4,1,3,2,0:T(8,128)(2,1)S(1)}, u32[]{:S(2)}, u32[]{:S(2)}) collective-permute-start(bf16[1,8,2,3,512]{4,1,3,2,0:T(8,128)(2,1)S(1)} %collective-permute-done.3), channel_id=1, source_target_pairs={{0,14},{2,0},{4,2},{6,4},{8,6},{10,8},{12,10},{14,12},{1,15},{3,1}... | collective-permute-start | bytes 147464 | tf_op jit(solution)/shard_map/ppermute | solution.py:92
  29.4 36.8 %collective-permute-start.6 = (bf16[1,8,2,3,512]{4,1,3,2,0:T(8,128)(2,1)S(1)}, bf16[1,8,2,3,512]{4,1,3,2,0:T(8,128)(2,1)S(1)}, u32[]{:S(2)}, u32[]{:S(2)}) collective-permute-start(bf16[1,8,2,3,512]{4,1,3,2,0:T(8,128)(2,1)S(1)} %collective-permute-done.4), channel_id=1, source_target_pairs={{0,2},{2,4},{4,6},{6,8},{8,10},{10,12},{12,14},{14,0},{1,3},{3,5},... | collective-permute-start | bytes 147464 | tf_op jit(solution)/shard_map/ppermute | solution.py:87
  72.9 8.5 %collective-permute-start.7 = (bf16[1,32,2,3,512]{4,1,3,2,0:T(8,128)(2,1)}, bf16[1,32,2,3,512]{4,1,3,2,0:T(8,128)(2,1)}, u32[]{:S(2)}, u32[]{:S(2)}) collective-permute-start(bf16[1,32,2,3,512]{4,1,3,2,0:T(8,128)(2,1)} %copy.40), channel_id=1, source_target_pairs={{0,1},{2,3},{4,5},{6,7},{8,9},{10,11},{12,13},{14,15},{16,17},{18,... | collective-permute-start | bytes 589832 | tf_op jit(solution)/shard_map/ppermute | solution.py:15
  75.8 6.9 %collective-permute-start.8 = (bf16[1,32,2,3,512]{4,1,3,2,0:T(8,128)(2,1)}, bf16[1,32,2,3,512]{4,1,3,2,0:T(8,128)(2,1)}, u32[]{:S(2)}, u32[]{:S(2)}) collective-permute-start(bf16[1,32,2,3,512]{4,1,3,2,0:T(8,128)(2,1)} %copy.41), channel_id=1, source_target_pairs={{1,0},{3,2},{5,4},{7,6},{9,8},{11,10},{13,12},{15,14},{17,16},{19,... | collective-permute-start | bytes 589832 | tf_op jit(solution)/shard_map/ppermute | solution.py:17
  92.2 1.9 %copy-start.1 = (bf16[2,128,2,8,128,1,1]{4,3,1,2,0,6,5:T(8,128)(2,1)S(1)}, bf16[2,128,2,8,128,1,1]{4,3,1,2,0,6,5:T(8,128)(2,1)}, u32[]{:S(2)}) copy-start(bf16[2,128,2,8,128,1,1]{4,3,1,2,0,6,5:T(8,128)(2,1)} %get-tuple-element.13) | copy-start | bytes 3145732
Sparse Core Ops, SparseCore 0:
  100.4 64.2 reduce-scatter.1
